TPU v7x, 32 devices: a whole 2x2x4 slice. The times are simulated.
32 devices in a mesh: ulysses: 4 (over x, core), context: 8 (over z, y).
Axes of the slice: x: 2, y: 2, z: 4, core: 2. Of those that a mesh axis runs over, the one named last changes fastest.
Arguments:
- queries: bfloat16 [4096, 2048], P(('context', 'ulysses')), may hold values from -6 to 6
- key_rows: bfloat16 [4096, 2048], P(('context', 'ulysses')), may hold values from -6 to 6
- value_rows: bfloat16 [4096, 2048], P(('context', 'ulysses')), may hold values from -6 to 6
- grad_out: bfloat16 [4096, 2048], P(('context', 'ulysses')), may hold values from -6 to 6
Outputs:
- attended: bfloat16 [4096, 2048], P(('context', 'ulysses'))
- grad_queries: bfloat16 [4096, 2048], P(('context', 'ulysses'))
- grad_keys: bfloat16 [4096, 2048], P(('context', 'ulysses'))
- grad_values: bfloat16 [4096, 2048], P(('context', 'ulysses'))
All inputs are finite; a program needn't handle non-finite values.
Results may differ from a plain program's by a relative error of at most 0.03.
Values may be sent and summed in bfloat16 or wider, within the bound.
No kernel may reach another device: no remote copies, remote signals or barrier semaphores. Data moves between devices by JAX's collectives and lax.ppermute only.
A program may use at most 128 MiB of HBM per device.

v0:
```python
import jax
import jax.numpy as jnp
from jax import lax
from jax.sharding import PartitionSpec as P

HEAD_DIM = 128


def swapped(x, axis, distance):
    return lax.ppermute(x, axis, [(i, i ^ 1 << distance) for i in range(lax.axis_size(axis))])


def split_heads(flat_rows):
    return flat_rows.reshape(flat_rows.shape[0], flat_rows.shape[1] // HEAD_DIM, HEAD_DIM)


def join_heads(head_rows):
    return head_rows.reshape(head_rows.shape[0], head_rows.shape[1] * head_rows.shape[2])


def block_forward(query3, key3, value3):
    softmax_scale = HEAD_DIM ** (-0.5)
    logit_scores = (
        jnp.einsum("qhd,khd->hqk", query3, key3, preferred_element_type=jnp.float32) * softmax_scale
    )
    row_peak = jnp.max(logit_scores, axis=-1)
    shifted = jnp.exp(logit_scores - row_peak[:, :, None])
    row_total = jnp.sum(shifted, axis=-1)
    partial_out = jnp.einsum(
        "hqk,khd->qhd", shifted.astype(jnp.bfloat16), value3, preferred_element_type=jnp.float32
    )
    return (row_peak, row_total, partial_out)


def merge_block(running, fresh):
    run_peak, run_total, run_out = running
    new_peak, new_total, new_out = fresh
    joined_peak = jnp.maximum(run_peak, new_peak)
    old_factor = jnp.exp(run_peak - joined_peak)
    new_factor = jnp.exp(new_peak - joined_peak)
    joined_total = old_factor * run_total + new_factor * new_total
    joined_out = run_out * old_factor.T[:, :, None] + new_out * new_factor.T[:, :, None]
    return (joined_peak, joined_total, joined_out)


def block_backward(query3, grad3, key3, value3, log_norm, dot_term):
    softmax_scale = HEAD_DIM ** (-0.5)
    logit_scores = (
        jnp.einsum("qhd,khd->hqk", query3, key3, preferred_element_type=jnp.float32) * softmax_scale
    )
    probs = jnp.exp(logit_scores - log_norm[:, :, None])
    value_term = jnp.einsum(
        "hqk,qhd->khd", probs.astype(jnp.bfloat16), grad3, preferred_element_type=jnp.float32
    ).astype(jnp.bfloat16)
    probability_gradient = jnp.einsum(
        "qhd,khd->hqk", grad3, value3, preferred_element_type=jnp.float32
    )
    score_gradient = (probs * (probability_gradient - dot_term[:, :, None]) * softmax_scale).astype(
        jnp.bfloat16
    )
    query_term = jnp.einsum(
        "hqk,khd->qhd", score_gradient, key3, preferred_element_type=jnp.float32
    ).astype(jnp.bfloat16)
    key_term = jnp.einsum(
        "hqk,qhd->khd", score_gradient, query3, preferred_element_type=jnp.float32
    ).astype(jnp.bfloat16)
    return (query_term, key_term, value_term)


def body(queries, key_rows, value_rows, grad_out):
    levels = lax.axis_size("context").bit_length() - 1
    query_flat, key_flat, value_flat, grad_flat = (
        lax.all_to_all(queries, "ulysses", split_axis=1, concat_axis=0, tiled=True),
        lax.all_to_all(key_rows, "ulysses", split_axis=1, concat_axis=0, tiled=True),
        lax.all_to_all(value_rows, "ulysses", split_axis=1, concat_axis=0, tiled=True),
        lax.all_to_all(grad_out, "ulysses", split_axis=1, concat_axis=0, tiled=True),
    )
    query3 = split_heads(query_flat)
    key3 = split_heads(key_flat)
    value3 = split_heads(value_flat)
    grad3 = split_heads(grad_flat)
    running = block_forward(query3, key3, value3)
    cached = []
    for level in range(levels):
        remote_key, remote_value = swapped((key_flat, value_flat), "context", level)
        cached.append((remote_key, remote_value))
        running = merge_block(
            running, block_forward(query3, split_heads(remote_key), split_heads(remote_value))
        )
    run_peak, run_total, run_out = running
    output3 = (run_out / run_total.T[:, :, None]).astype(jnp.bfloat16)
    log_norm = run_peak + jnp.log(run_total)
    dot_term = jnp.sum(grad3.astype(jnp.float32) * output3.astype(jnp.float32), axis=-1).T
    own_terms = block_backward(query3, grad3, key3, value3, log_norm, dot_term)
    grad_query = own_terms[0].astype(jnp.float32)
    grad_key = own_terms[1].astype(jnp.float32)
    grad_value = own_terms[2].astype(jnp.float32)
    for level in range(levels):
        remote_key, remote_value = swapped((key_flat, value_flat), "context", level)
        terms = block_backward(
            query3, grad3, split_heads(remote_key), split_heads(remote_value), log_norm, dot_term
        )
        grad_query = grad_query + terms[0].astype(jnp.float32)
        outgoing = (terms[1], terms[2])
        returned = swapped((outgoing[0], outgoing[1]), "context", level)
        grad_key = grad_key + returned[0].astype(jnp.float32)
        grad_value = grad_value + returned[1].astype(jnp.float32)
    results = (
        lax.all_to_all(join_heads(output3), "ulysses", split_axis=0, concat_axis=1, tiled=True),
        lax.all_to_all(
            join_heads(grad_query.astype(jnp.bfloat16)),
            "ulysses",
            split_axis=0,
            concat_axis=1,
            tiled=True,
        ),
        lax.all_to_all(
            join_heads(grad_key.astype(jnp.bfloat16)),
            "ulysses",
            split_axis=0,
            concat_axis=1,
            tiled=True,
        ),
        lax.all_to_all(
            join_heads(grad_value.astype(jnp.bfloat16)),
            "ulysses",
            split_axis=0,
            concat_axis=1,
            tiled=True,
        ),
    )
    return (results[0], results[1], results[2], results[3])


def solution(mesh):
    placed = (
        P(("context", "ulysses"), None),
        P(("context", "ulysses"), None),
        P(("context", "ulysses"), None),
        P(("context", "ulysses"), None),
    )
    return jax.shard_map(
        body,
        mesh=mesh,
        in_specs=placed,
        out_specs=(
            P(("context", "ulysses"), None),
            P(("context", "ulysses"), None),
            P(("context", "ulysses"), None),
            P(("context", "ulysses"), None),
        ),
        check_vma=False,
    )
```

profile of v0, /device:TPU:0, one launch (start us, length us, event | category | flops | bytes accessed | tf_op | source)
XLA Modules:
  0.0 214.5 jit_solution(4984784563907744337)
XLA Ops:
  2.6 4.2 %all-to-all-start = ((bf16[128,4,512]{2,0,1:T(8,128)(2,1)}), bf16[128,4,512]{2,0,1:T(8,128)(2,1)S(1)}, u32[]{:S(2)}, u32[]{:S(2)}) async-start(bf16[128,4,512]{2,0,1:T(8,128)(2,1)} %bitcast.183), calls=%async_computation | async-start | bytes 1048576 | tf_op jit(solution)/shard_map/all_to_all | solution.py:73
  6.9 2.0 copy.207
  8.9 6.8 %all-to-all-done = bf16[128,4,512]{2,0,1:T(8,128)(2,1)S(1)} async-done(((bf16[128,4,512]{2,0,1:T(8,128)(2,1)}), bf16[128,4,512]{2,0,1:T(8,128)(2,1)S(1)}, u32[]{:S(2)}, u32[]{:S(2)}) %all-to-all-start) | async-done | bytes 524320 | tf_op jit(solution)/shard_map/all_to_all | solution.py:73
  15.7 3.5 %all-to-all-start.1 = ((bf16[128,4,512]{0,2,1:T(8,128)(2,1)}), bf16[128,4,512]{0,2,1:T(8,128)(2,1)S(1)}, u32[]{:S(2)}, u32[]{:S(2)}) async-start(bf16[128,4,512]{0,2,1:T(8,128)(2,1)} %bitcast.1), calls=%async_computation.1 | async-start | bytes 1048576 | tf_op jit(solution)/shard_map/all_to_all | solution.py:74
  20.2 7.8 %all-to-all-done.1 = bf16[128,4,512]{0,2,1:T(8,128)(2,1)S(1)} async-done(((bf16[128,4,512]{0,2,1:T(8,128)(2,1)}), bf16[128,4,512]{0,2,1:T(8,128)(2,1)S(1)}, u32[]{:S(2)}, u32[]{:S(2)}) %all-to-all-start.1) | async-done | bytes 524320 | tf_op jit(solution)/shard_map/all_to_all | solution.py:74
  27.9 3.5 %all-to-all-start.2 = ((bf16[128,4,512]{0,2,1:T(8,128)(2,1)}), bf16[128,4,512]{0,2,1:T(8,128)(2,1)S(1)}, u32[]{:S(2)}, u32[]{:S(2)}) async-start(bf16[128,4,512]{0,2,1:T(8,128)(2,1)} %bitcast.3), calls=%async_computation.2 | async-start | bytes 1048576 | tf_op jit(solution)/shard_map/all_to_all | solution.py:75
  31.6 2.3 %collective-permute-start = (bf16[512,512]{1,0:T(8,128)(2,1)S(1)}, bf16[512,512]{1,0:T(8,128)(2,1)}, u32[]{:S(2)}, u32[]{:S(2)}) collective-permute-start(bf16[512,512]{1,0:T(8,128)(2,1)S(1)} %bitcast.197), channel_id=1, source_target_pairs={{0,1},{1,0},{2,3},{3,2},{4,5},{5,4},{6,7},{7,6},{8,9},{9,8},{10,11... | collective-permute-start | bytes 1572872 | tf_op jit(solution)/shard_map/ppermute | solution.py:10
  34.9 5.3 %all-to-all-done.2 = bf16[128,4,512]{0,2,1:T(8,128)(2,1)S(1)} async-done(((bf16[128,4,512]{0,2,1:T(8,128)(2,1)}), bf16[128,4,512]{0,2,1:T(8,128)(2,1)S(1)}, u32[]{:S(2)}, u32[]{:S(2)}) %all-to-all-start.2) | async-done | bytes 524320 | tf_op jit(solution)/shard_map/all_to_all | solution.py:75
  40.2 3.5 %all-to-all-start.4 = ((bf16[128,4,512]{0,2,1:T(8,128)(2,1)}), bf16[128,4,512]{0,2,1:T(8,128)(2,1)S(1)}, u32[]{:S(2)}, u32[]{:S(2)}) async-start(bf16[128,4,512]{0,2,1:T(8,128)(2,1)} %bitcast.29), calls=%async_computation.4 | async-start | bytes 1048576 | tf_op jit(solution)/shard_map/all_to_all | solution.py:76
  44.8 3.3 %collective-permute-start.5 = (bf16[512,512]{1,0:T(8,128)(2,1)}, bf16[512,512]{1,0:T(8,128)(2,1)}, u32[]{:S(2)}, u32[]{:S(2)}) collective-permute-start(bf16[512,512]{1,0:T(8,128)(2,1)} %bitcast.11), channel_id=1, source_target_pairs={{0,4},{1,5},{2,6},{3,7},{4,0},{5,1},{6,2},{7,3},{8,12},{9,13},{10,... | collective-permute-start | bytes 1572872 | tf_op jit(solution)/shard_map/ppermute | solution.py:10
  51.8 2.7 %multiply_reduce_fusion.3 = (f32[4,512]{1,0:T(4,128)S(1)}, f32[4,512,512]{1,2,0:T(8,128)}) fusion(bf16[512,4,128]{2,1,0:T(4,128)(2,1)S(1)} %reshape.135, bf16[512,4,128]{2,1,0:T(4,128)(2,1)S(1)} %reshape.134), kind=kOutput, calls=%fused_computation.27 | convolution fusion | flops 270530560 | bytes 5251072 | tf_op jit(solution)/shard_map/qhd,khd->hqk/dot_general | solution.py:24
  59.2 2.8 %multiply_reduce_fusion.2 = (f32[4,512]{1,0:T(4,128)S(1)}, f32[4,512,512]{1,2,0:T(8,128)}) fusion(bf16[512,4,128]{0,2,1:T(8,128)(2,1)S(1)} %bitcast.184, bf16[512,4,128]{2,1,0:T(4,128)(2,1)S(1)} %reshape.134), kind=kOutput, calls=%fused_computation.26 | convolution fusion | flops 270530560 | bytes 5251072 | tf_op jit(solution)/shard_map/qhd,khd->hqk/dot_general | solution.py:24
  62.0 33.0 %collective-permute-done.2 = bf16[512,512]{1,0:T(8,128)(2,1)} collective-permute-done((bf16[512,512]{1,0:T(8,128)(2,1)S(1)}, bf16[512,512]{1,0:T(8,128)(2,1)}, u32[]{:S(2)}, u32[]{:S(2)}) %collective-permute-start.2) | collective-permute-done | bytes 524320 | tf_op jit(solution)/shard_map/ppermute | solution.py:10
  96.2 2.8 %multiply_reduce_fusion.1 = (f32[4,512]{1,0:T(4,128)S(1)}, f32[4,512,512]{1,2,0:T(8,128)}) fusion(bf16[512,4,128]{0,2,1:T(8,128)(2,1)S(1)} %bitcast.186, bf16[512,4,128]{2,1,0:T(4,128)(2,1)S(1)} %reshape.134), kind=kOutput, calls=%fused_computation.25 | convolution fusion | flops 270530560 | bytes 5251072 | tf_op jit(solution)/shard_map/qhd,khd->hqk/dot_general | solution.py:24
  101.1 3.1 %copy-done.2 = f32[4,512,512]{1,2,0:T(8,128)S(1)} copy-done((f32[4,512,512]{1,2,0:T(8,128)S(1)}, f32[4,512,512]{1,2,0:T(8,128)}, u32[]{:S(2)}) %copy-start.2) | copy-done | bytes 4194328
  113.9 4.2 %fusion.74 = f32[512,4,128]{0,2,1:T(8,128)} fusion(bf16[512,4,128]{0,2,1:T(8,128)(2,1)S(1)} %bitcast.190, f32[4,512,512]{1,2,0:T(8,128)} %get-tuple-element.26, f32[4,512]{1,0:T(4,128)S(1)} %get-tuple-element.25, f32[512,4]{0,1:T(4,128)S(1)} %get-tuple-element.21), kind=kOutput, calls=%fused_computation.62 | convolution fusion | flops 271843328 | bytes 5783552 | tf_op jit(solution)/shard_map/hqk,khd->qhd/dot_general | solution.py:29
  122.9 4.1 %fusion.80 = f32[512,4,128]{0,2,1:T(8,128)} fusion(bf16[512,4,128]{0,2,1:T(8,128)(2,1)S(1)} %bitcast.192, f32[4,512,512]{1,2,0:T(8,128)} %copy-done.5, f32[4,512]{1,0:T(4,128)S(1)} %get-tuple-element.23, f32[512,4]{0,1:T(4,128)S(1)} %get-tuple-element.22), kind=kOutput, calls=%fused_computation.64 | convolution fusion | flops 271843328 | bytes 5783552 | tf_op jit(solution)/shard_map/hqk,khd->qhd/dot_general | solution.py:29
  128.3 5.2 %multiply_reduce_fusion.4 = (f32[512,4]{0,1:T(4,128)S(1)}, bf16[512,4,128]{0,2,1:T(8,128)(2,1)}) fusion(bf16[512,4,128]{0,2,1:T(8,128)(2,1)S(1)} %reshape.143, f32[512,4]{0,1:T(4,128)S(1)} %get-tuple-element.16, f32[512,4,128]{0,2,1:T(8,128)} %fusion.80, f32[512,4]{0,1:T(4,128)S(1)} %get-tuple-element.19, f32[512,4,128]{0,2,1:T(8,128)} %fusion.74, ...), kind=kOutput, calls=%fused_computation.98 | convolution fusion | flops 274724864 | bytes 8962048 | tf_op jit(solution)/shard_map/hqk,khd->qhd/dot_general | solution.py:29
  146.1 2.6 %collective-permute-start.10 = (bf16[512,4,128]{2,0,1:T(8,128)(2,1)}, bf16[512,4,128]{2,0,1:T(8,128)(2,1)}, u32[]{:S(2)}, u32[]{:S(2)}) collective-permute-start(bf16[512,4,128]{2,0,1:T(8,128)(2,1)} %fusion.118), channel_id=1, source_target_pairs={{0,2},{1,3},{2,0},{3,1},{4,6},{5,7},{6,4},{7,5},{8,10},{9,11},{10,... | collective-permute-start | bytes 1572872 | tf_op jit(solution)/shard_map/ppermute | solution.py:10
  156.5 4.1 %all-to-all-start.5 = ((bf16[4,128,512]{2,1,0:T(8,128)(2,1)}), bf16[4,128,512]{2,1,0:T(8,128)(2,1)}, u32[]{:S(2)}, u32[]{:S(2)}) async-start(bf16[4,128,512]{2,1,0:T(8,128)(2,1)} %all_to_all.126), calls=%async_computation.5 | async-start | bytes 1048576 | tf_op jit(solution)/shard_map/all_to_all | solution.py:110
  160.6 3.1 %fusion.112 = bf16[512,4,128]{2,0,1:T(8,128)(2,1)} fusion(bf16[4,512,512]{1,2,0:T(8,128)(2,1)} %copy-done.11, bf16[512,4,128]{2,1,0:T(4,128)(2,1)S(1)} %reshape.134), kind=kOutput, calls=%fused_computation.90 | convolution fusion | flops 268697600 | bytes 3145728 | tf_op jit(solution)/shard_map/hqk,qhd->khd/dot_general | solution.py:64
  164.3 3.1 %fusion.113 = bf16[512,4,128]{2,0,1:T(8,128)(2,1)} fusion(bf16[4,512,512]{1,2,0:T(8,128)(2,1)} %copy-done.10, bf16[512,4,128]{2,1,0:T(4,128)(2,1)S(1)} %reshape.134), kind=kOutput, calls=%fused_computation.91 | convolution fusion | flops 268697600 | bytes 3145728 | tf_op jit(solution)/shard_map/hqk,qhd->khd/dot_general | solution.py:64
  167.4 3.8 %collective-permute-done.11 = bf16[512,4,128]{2,0,1:T(8,128)(2,1)} collective-permute-done((bf16[512,4,128]{2,0,1:T(8,128)(2,1)}, bf16[512,4,128]{2,0,1:T(8,128)(2,1)}, u32[]{:S(2)}, u32[]{:S(2)}) %collective-permute-start.11) | collective-permute-done | bytes 524320 | tf_op jit(solution)/shard_map/ppermute | solution.py:10
  175.1 4.1 %all-to-all-start.3 = ((bf16[4,128,512]{1,2,0:T(8,128)(2,1)}), bf16[4,128,512]{1,2,0:T(8,128)(2,1)}, u32[]{:S(2)}, u32[]{:S(2)}) async-start(bf16[4,128,512]{1,2,0:T(8,128)(2,1)} %copy.231), calls=%async_computation.3 | async-start | bytes 1048576 | tf_op jit(solution)/shard_map/all_to_all | solution.py:109
  179.2 3.6 %add_convert_fusion = bf16[512,4,128]{2,0,1:T(8,128)(2,1)S(1)} fusion(bf16[512,4,128]{2,0,1:T(8,128)(2,1)} %collective-permute-done.11, bf16[512,4,128]{2,0,1:T(8,128)(2,1)} %collective-permute-done.10, bf16[512,4,128]{2,0,1:T(8,128)(2,1)} %collective-permute-done.9, bf16[512,4,128]{0,2,1:T(8,128)(2,1)S(1)} %reshape.143, ...), kind=kOutput, calls=%fused_computation.96 | convolution fusion | flops 273940480 | bytes 6823936 | tf_op jit(solution)/shard_map/hqk,qhd->khd/dot_general | solution.py:52
  184.3 3.8 %all-to-all-done.3 = bf16[4,128,512]{1,2,0:T(8,128)(2,1)} async-done(((bf16[4,128,512]{1,2,0:T(8,128)(2,1)}), bf16[4,128,512]{1,2,0:T(8,128)(2,1)}, u32[]{:S(2)}, u32[]{:S(2)}) %all-to-all-start.3) | async-done | bytes 524320 | tf_op jit(solution)/shard_map/all_to_all | solution.py:109
  188.1 3.5 %all-to-all-start.7 = ((bf16[4,128,512]{2,1,0:T(8,128)(2,1)}), bf16[4,128,512]{2,1,0:T(8,128)(2,1)S(1)}, u32[]{:S(2)}, u32[]{:S(2)}) async-start(bf16[4,128,512]{2,1,0:T(8,128)(2,1)} %all_to_all.134), calls=%async_computation.7 | async-start | bytes 1048576 | tf_op jit(solution)/shard_map/all_to_all | solution.py:124
  191.6 5.9 %collective-permute-done.8 = bf16[512,4,128]{2,0,1:T(8,128)(2,1)} collective-permute-done((bf16[512,4,128]{2,0,1:T(8,128)(2,1)}, bf16[512,4,128]{2,0,1:T(8,128)(2,1)}, u32[]{:S(2)}, u32[]{:S(2)}) %collective-permute-start.8) | collective-permute-done | bytes 524320 | tf_op jit(solution)/shard_map/ppermute | solution.py:10
  197.5 2.1 add_convert_fusion.1
  201.0 3.5 %all-to-all-start.6 = ((bf16[4,128,512]{2,1,0:T(8,128)(2,1)}), bf16[4,128,512]{2,1,0:T(8,128)(2,1)S(1)}, u32[]{:S(2)}, u32[]{:S(2)}) async-start(bf16[4,128,512]{2,1,0:T(8,128)(2,1)} %all_to_all.130), calls=%async_computation.6 | async-start | bytes 1048576 | tf_op jit(solution)/shard_map/all_to_all | solution.py:117
  206.8 2.0 copy.268
  210.1 3.1 %all-to-all-done.6 = bf16[4,128,512]{2,1,0:T(8,128)(2,1)S(1)} async-done(((bf16[4,128,512]{2,1,0:T(8,128)(2,1)}), bf16[4,128,512]{2,1,0:T(8,128)(2,1)S(1)}, u32[]{:S(2)}, u32[]{:S(2)}) %all-to-all-start.6) | async-done | bytes 524320 | tf_op jit(solution)/shard_map/all_to_all | solution.py:117
  (117 shorter events, 65.1 us)
Async XLA Ops:
  0.6 18.5 %copy-start.22 = (bf16[128,2048]{1,0:T(8,128)(2,1)S(1)}, bf16[128,2048]{1,0:T(8,128)(2,1)}, u32[]{:S(2)}) copy-start(bf16[128,2048]{1,0:T(8,128)(2,1)} %param.6) | copy-start | bytes 1572868
  0.6 33.3 %copy-start.23 = (bf16[128,2048]{1,0:T(8,128)(2,1)S(1)}, bf16[128,2048]{1,0:T(8,128)(2,1)}, u32[]{:S(2)}) copy-start(bf16[128,2048]{1,0:T(8,128)(2,1)} %param.7) | copy-start | bytes 1572868
  2.6 13.1 %all-to-all-start = ((bf16[128,4,512]{2,0,1:T(8,128)(2,1)}), bf16[128,4,512]{2,0,1:T(8,128)(2,1)S(1)}, u32[]{:S(2)}, u32[]{:S(2)}) async-start(bf16[128,4,512]{2,0,1:T(8,128)(2,1)} %bitcast.183), calls=%async_computation | async-start | bytes 1048576 | tf_op jit(solution)/shard_map/all_to_all | solution.py:73
  15.7 12.3 %all-to-all-start.1 = ((bf16[128,4,512]{0,2,1:T(8,128)(2,1)}), bf16[128,4,512]{0,2,1:T(8,128)(2,1)S(1)}, u32[]{:S(2)}, u32[]{:S(2)}) async-start(bf16[128,4,512]{0,2,1:T(8,128)(2,1)} %bitcast.1), calls=%async_computation.1 | async-start | bytes 1048576 | tf_op jit(solution)/shard_map/all_to_all | solution.py:74
  27.9 12.3 %all-to-all-start.2 = ((bf16[128,4,512]{0,2,1:T(8,128)(2,1)}), bf16[128,4,512]{0,2,1:T(8,128)(2,1)S(1)}, u32[]{:S(2)}, u32[]{:S(2)}) async-start(bf16[128,4,512]{0,2,1:T(8,128)(2,1)} %bitcast.3), calls=%async_computation.2 | async-start | bytes 1048576 | tf_op jit(solution)/shard_map/all_to_all | solution.py:75
  31.6 25.9 %collective-permute-start = (bf16[512,512]{1,0:T(8,128)(2,1)S(1)}, bf16[512,512]{1,0:T(8,128)(2,1)}, u32[]{:S(2)}, u32[]{:S(2)}) collective-permute-start(bf16[512,512]{1,0:T(8,128)(2,1)S(1)} %bitcast.197), channel_id=1, source_target_pairs={{0,1},{1,0},{2,3},{3,2},{4,5},{5,4},{6,7},{7,6},{8,9},{9,8},{10,11... | collective-permute-start | bytes 1572872 | tf_op jit(solution)/shard_map/ppermute | solution.py:10
  40.2 16.7 %all-to-all-start.4 = ((bf16[128,4,512]{0,2,1:T(8,128)(2,1)}), bf16[128,4,512]{0,2,1:T(8,128)(2,1)S(1)}, u32[]{:S(2)}, u32[]{:S(2)}) async-start(bf16[128,4,512]{0,2,1:T(8,128)(2,1)} %bitcast.29), calls=%async_computation.4 | async-start | bytes 1048576 | tf_op jit(solution)/shard_map/all_to_all | solution.py:76
  43.8 11.9 %copy-start.12 = (bf16[512,4,128]{2,1,0:T(4,128)(2,1)}, bf16[512,4,128]{2,1,0:T(4,128)(2,1)S(1)}, u32[]{:S(2)}) copy-start(bf16[512,4,128]{2,1,0:T(4,128)(2,1)S(1)} %reshape.135) | copy-start | bytes 1572868
  44.8 76.8 %collective-permute-start.5 = (bf16[512,512]{1,0:T(8,128)(2,1)}, bf16[512,512]{1,0:T(8,128)(2,1)}, u32[]{:S(2)}, u32[]{:S(2)}) collective-permute-start(bf16[512,512]{1,0:T(8,128)(2,1)} %bitcast.11), channel_id=1, source_target_pairs={{0,4},{1,5},{2,6},{3,7},{4,0},{5,1},{6,2},{7,3},{8,12},{9,13},{10,... | collective-permute-start | bytes 1572872 | tf_op jit(solution)/shard_map/ppermute | solution.py:10
  48.1 64.5 %collective-permute-start.3 = (bf16[512,512]{1,0:T(8,128)(2,1)}, bf16[512,512]{1,0:T(8,128)(2,1)}, u32[]{:S(2)}, u32[]{:S(2)}) collective-permute-start(bf16[512,512]{1,0:T(8,128)(2,1)} %bitcast.11), channel_id=1, source_target_pairs={{0,2},{1,3},{2,0},{3,1},{4,6},{5,7},{6,4},{7,5},{8,10},{9,11},{10,... | collective-permute-start | bytes 1572872 | tf_op jit(solution)/shard_map/ppermute | solution.py:10
  49.7 77.3 %collective-permute-start.1 = (bf16[512,512]{1,0:T(8,128)(2,1)}, bf16[512,512]{1,0:T(8,128)(2,1)}, u32[]{:S(2)}, u32[]{:S(2)}) collective-permute-start(bf16[512,512]{1,0:T(8,128)(2,1)} %bitcast.11), channel_id=1, source_target_pairs={{0,1},{1,0},{2,3},{3,2},{4,5},{5,4},{6,7},{7,6},{8,9},{9,8},{10,11... | collective-permute-start | bytes 1572872 | tf_op jit(solution)/shard_map/ppermute | solution.py:10
  51.2 43.8 %collective-permute-start.2 = (bf16[512,512]{1,0:T(8,128)(2,1)S(1)}, bf16[512,512]{1,0:T(8,128)(2,1)}, u32[]{:S(2)}, u32[]{:S(2)}) collective-permute-start(bf16[512,512]{1,0:T(8,128)(2,1)S(1)} %bitcast.198), channel_id=1, source_target_pairs={{0,2},{1,3},{2,0},{3,1},{4,6},{5,7},{6,4},{7,5},{8,10},{9,11},{10,... | collective-permute-start | bytes 1572872 | tf_op jit(solution)/shard_map/ppermute | solution.py:10
  56.9 53.8 %copy-start.16 = (bf16[512,4,128]{0,2,1:T(8,128)(2,1)}, bf16[512,4,128]{0,2,1:T(8,128)(2,1)S(1)}, u32[]{:S(2)}) copy-start(bf16[512,4,128]{0,2,1:T(8,128)(2,1)S(1)} %reshape.136) | copy-start | bytes 1572868
  57.5 41.5 %collective-permute-start.4 = (bf16[512,512]{1,0:T(8,128)(2,1)S(1)}, bf16[512,512]{1,0:T(8,128)(2,1)}, u32[]{:S(2)}, u32[]{:S(2)}) collective-permute-start(bf16[512,512]{1,0:T(8,128)(2,1)S(1)} %bitcast.199), channel_id=1, source_target_pairs={{0,4},{1,5},{2,6},{3,7},{4,0},{5,1},{6,2},{7,3},{8,12},{9,13},{10,... | collective-permute-start | bytes 1572872 | tf_op jit(solution)/shard_map/ppermute | solution.py:10
  59.2 39.8 %copy-start.14 = (bf16[512,512]{0,1:T(8,128)(2,1)}, bf16[512,512]{0,1:T(8,128)(2,1)S(1)}, u32[]{:S(2)}) copy-start(bf16[512,512]{0,1:T(8,128)(2,1)S(1)} %copy.216) | copy-start | bytes 1572868
  100.3 5.3 %copy-start.20 = (bf16[512,512]{0,1:T(8,128)(2,1)}, bf16[512,512]{0,1:T(8,128)(2,1)S(1)}, u32[]{:S(2)}) copy-start(bf16[512,512]{0,1:T(8,128)(2,1)S(1)} %copy.226) | copy-start | bytes 1572868
  113.9 6.1 %copy-start.6 = (f32[4,512,512]{1,2,0:T(8,128)S(1)}, f32[4,512,512]{1,2,0:T(8,128)}, u32[]{:S(2)}) copy-start(f32[4,512,512]{1,2,0:T(8,128)} %copy-done.5) | copy-start | bytes 12582916
  135.6 16.5 %copy-start.11 = (bf16[4,512,512]{1,2,0:T(8,128)(2,1)}, bf16[4,512,512]{1,2,0:T(8,128)(2,1)S(1)}, u32[]{:S(2)}) copy-start(bf16[4,512,512]{1,2,0:T(8,128)(2,1)S(1)} %multiply_convert_fusion.2) | copy-start | bytes 6291460
  138.6 12.6 %copy-start.10 = (bf16[4,512,512]{1,2,0:T(8,128)(2,1)}, bf16[4,512,512]{1,2,0:T(8,128)(2,1)S(1)}, u32[]{:S(2)}) copy-start(bf16[4,512,512]{1,2,0:T(8,128)(2,1)S(1)} %multiply_convert_fusion.1) | copy-start | bytes 6291460
  143.1 7.1 %copy-start.13 = (bf16[512,4,128]{2,1,0:T(4,128)(2,1)S(1)}, bf16[512,4,128]{2,1,0:T(4,128)(2,1)}, u32[]{:S(2)}) copy-start(bf16[512,4,128]{2,1,0:T(4,128)(2,1)} %copy-done.12) | copy-start | bytes 1572868
  144.6 6.5 %copy-start.19 = (bf16[512,512]{0,1:T(8,128)(2,1)S(1)}, bf16[512,512]{0,1:T(8,128)(2,1)}, u32[]{:S(2)}) copy-start(bf16[512,512]{0,1:T(8,128)(2,1)} %copy-done.18) | copy-start | bytes 1572868
  145.5 6.6 %copy-start.15 = (bf16[512,512]{0,1:T(8,128)(2,1)S(1)}, bf16[512,512]{0,1:T(8,128)(2,1)}, u32[]{:S(2)}) copy-start(bf16[512,512]{0,1:T(8,128)(2,1)} %copy-done.14) | copy-start | bytes 1572868
  145.5 25.7 %collective-permute-start.11 = (bf16[512,4,128]{2,0,1:T(8,128)(2,1)}, bf16[512,4,128]{2,0,1:T(8,128)(2,1)}, u32[]{:S(2)}, u32[]{:S(2)}) collective-permute-start(bf16[512,4,128]{2,0,1:T(8,128)(2,1)} %fusion.115), channel_id=1, source_target_pairs={{0,4},{1,5},{2,6},{3,7},{4,0},{5,1},{6,2},{7,3},{8,12},{9,13},{10,... | collective-permute-start | bytes 1572872 | tf_op jit(solution)/shard_map/ppermute | solution.py:10
  146.1 33.1 %collective-permute-start.10 = (bf16[512,4,128]{2,0,1:T(8,128)(2,1)}, bf16[512,4,128]{2,0,1:T(8,128)(2,1)}, u32[]{:S(2)}, u32[]{:S(2)}) collective-permute-start(bf16[512,4,128]{2,0,1:T(8,128)(2,1)} %fusion.118), channel_id=1, source_target_pairs={{0,2},{1,3},{2,0},{3,1},{4,6},{5,7},{6,4},{7,5},{8,10},{9,11},{10,... | collective-permute-start | bytes 1572872 | tf_op jit(solution)/shard_map/ppermute | solution.py:10
  148.7 30.5 %collective-permute-start.9 = (bf16[512,4,128]{2,0,1:T(8,128)(2,1)}, bf16[512,4,128]{2,0,1:T(8,128)(2,1)}, u32[]{:S(2)}, u32[]{:S(2)}) collective-permute-start(bf16[512,4,128]{2,0,1:T(8,128)(2,1)} %fusion.121), channel_id=1, source_target_pairs={{0,1},{1,0},{2,3},{3,2},{4,5},{5,4},{6,7},{7,6},{8,9},{9,8},{10,11... | collective-permute-start | bytes 1572872 | tf_op jit(solution)/shard_map/ppermute | solution.py:10
  156.5 18.6 %all-to-all-start.5 = ((bf16[4,128,512]{2,1,0:T(8,128)(2,1)}), bf16[4,128,512]{2,1,0:T(8,128)(2,1)}, u32[]{:S(2)}, u32[]{:S(2)}) async-start(bf16[4,128,512]{2,1,0:T(8,128)(2,1)} %all_to_all.126), calls=%async_computation.5 | async-start | bytes 1048576 | tf_op jit(solution)/shard_map/all_to_all | solution.py:110
  163.8 27.8 %collective-permute-start.6 = (bf16[512,4,128]{2,0,1:T(8,128)(2,1)}, bf16[512,4,128]{2,0,1:T(8,128)(2,1)}, u32[]{:S(2)}, u32[]{:S(2)}) collective-permute-start(bf16[512,4,128]{2,0,1:T(8,128)(2,1)} %fusion.112), channel_id=1, source_target_pairs={{0,1},{1,0},{2,3},{3,2},{4,5},{5,4},{6,7},{7,6},{8,9},{9,8},{10,11... | collective-permute-start | bytes 1572872 | tf_op jit(solution)/shard_map/ppermute | solution.py:10
  167.4 24.2 %collective-permute-start.7 = (bf16[512,4,128]{2,0,1:T(8,128)(2,1)}, bf16[512,4,128]{2,0,1:T(8,128)(2,1)}, u32[]{:S(2)}, u32[]{:S(2)}) collective-permute-start(bf16[512,4,128]{2,0,1:T(8,128)(2,1)} %fusion.113), channel_id=1, source_target_pairs={{0,2},{1,3},{2,0},{3,1},{4,6},{5,7},{6,4},{7,5},{8,10},{9,11},{10,... | collective-permute-start | bytes 1572872 | tf_op jit(solution)/shard_map/ppermute | solution.py:10
  171.2 26.3 %collective-permute-start.8 = (bf16[512,4,128]{2,0,1:T(8,128)(2,1)}, bf16[512,4,128]{2,0,1:T(8,128)(2,1)}, u32[]{:S(2)}, u32[]{:S(2)}) collective-permute-start(bf16[512,4,128]{2,0,1:T(8,128)(2,1)} %fusion.114), channel_id=1, source_target_pairs={{0,4},{1,5},{2,6},{3,7},{4,0},{5,1},{6,2},{7,3},{8,12},{9,13},{10,... | collective-permute-start | bytes 1572872 | tf_op jit(solution)/shard_map/ppermute | solution.py:10
  175.1 13.0 %all-to-all-start.3 = ((bf16[4,128,512]{1,2,0:T(8,128)(2,1)}), bf16[4,128,512]{1,2,0:T(8,128)(2,1)}, u32[]{:S(2)}, u32[]{:S(2)}) async-start(bf16[4,128,512]{1,2,0:T(8,128)(2,1)} %copy.231), calls=%async_computation.3 | async-start | bytes 1048576 | tf_op jit(solution)/shard_map/all_to_all | solution.py:109
  188.1 12.9 %all-to-all-start.7 = ((bf16[4,128,512]{2,1,0:T(8,128)(2,1)}), bf16[4,128,512]{2,1,0:T(8,128)(2,1)S(1)}, u32[]{:S(2)}, u32[]{:S(2)}) async-start(bf16[4,128,512]{2,1,0:T(8,128)(2,1)} %all_to_all.134), calls=%async_computation.7 | async-start | bytes 1048576 | tf_op jit(solution)/shard_map/all_to_all | solution.py:124
  201.0 12.3 %all-to-all-start.6 = ((bf16[4,128,512]{2,1,0:T(8,128)(2,1)}), bf16[4,128,512]{2,1,0:T(8,128)(2,1)S(1)}, u32[]{:S(2)}, u32[]{:S(2)}) async-start(bf16[4,128,512]{2,1,0:T(8,128)(2,1)} %all_to_all.130), calls=%async_computation.6 | async-start | bytes 1048576 | tf_op jit(solution)/shard_map/all_to_all | solution.py:117
  (12 other events, 42.5 us)
where the time goes:
time: 216 us; the launch traced here: 215 us
  waiting for transfers between devices  69.5 us (32%)
  matrix products  52.5 us (24%)
  starting transfers between devices  44.6 us (21%)
  local copies, waits for them, and re-layouts  44 us (20%)
  other arithmetic  2.89 us (1%)
    ppermute x12, waiting for transfers between devices, swapped(): lax.ppermute(x, axis, [(i, i ^ 1 << distance) for i in range(lax.axis_siz...  42.7 us
    unnamed x55, local copies, waits for them, and re-layouts  18.2 us
    dot_general x4, matrix products, block_forward(): jnp.einsum('hqk,khd->qhd', shifted.astype(jnp.bfloat16), value3, preferre...  15.5 us
    ppermute x12, starting transfers between devices, swapped(): lax.ppermute(x, axis, [(i, i ^ 1 << distance) for i in range(lax.axis_siz...  14.7 us
    dot_general x4, matrix products, block_backward(): jnp.einsum('hqk,qhd->khd', score_gradient, query3, preferred_element_type...  9.81 us
    dot_general x4, matrix products, block_forward(): jnp.einsum('qhd,khd->hqk', query3, key3, preferred_element_type=jnp.float32)  8.99 us
    dot_general x4, matrix products, block_backward(): jnp.einsum('hqk,qhd->khd', probs.astype(jnp.bfloat16), grad3, preferred_e...  8.67 us
    all_to_all x1, waiting for transfers between devices, body(): lax.all_to_all(key_rows, 'ulysses', split_axis=1, concat_axis=0, tiled=True)  7.77 us
  transfers between devices with their start and end apart: 20, of which 8 were waited for; matrix products, arithmetic and copies ran while one was open for 31% of the time, Pallas kernels for 0%

commit v1 on v0

--- a/solution.py
+++ b/solution.py
@@ -4,6 +4,21 @@
 from jax.sharding import PartitionSpec as P
 
 HEAD_DIM = 128
+
+
+def stacks_all_attach(local_array, out_dim, base_x):
+    y2 = local_array.shape
+    return jnp.moveaxis(
+        local_array.reshape(*y2[:out_dim], base_x, y2[out_dim] // base_x, *y2[out_dim + 1 :]),
+        out_dim,
+        0,
+    )
+
+
+def frames_spread(original, pos_dim):
+    low = list(original.shape[1:])
+    low[pos_dim] *= original.shape[0]
+    return jnp.moveaxis(original, 0, pos_dim).reshape(low)
 
 
 def swapped(x, axis, distance):
@@ -69,8 +84,25 @@
 
 def body(queries, key_rows, value_rows, grad_out):
     levels = lax.axis_size("context").bit_length() - 1
+
+    def view_tails(my_tile, chip_axis, field, inputs):
+        answer = lax.axis_index(chip_axis)
+        v_next = lax.axis_size(chip_axis)
+        finding, t1 = (v_next, answer)
+        w2 = stacks_all_attach(my_tile, field, finding)
+        grid = [w2[t1]]
+        for i0 in range(1, finding):
+            block_now = w2[t1 ^ i0]
+            met_up = lax.ppermute(
+                block_now, chip_axis, perm=[(to_i, to_i ^ i0) for to_i in range(finding)]
+            )
+            grid.append(met_up)
+        wide_out = jnp.stack(grid, 0)
+        w2 = wide_out[t1 ^ jnp.arange(finding)]
+        return frames_spread(w2, inputs)
+
     query_flat, key_flat, value_flat, grad_flat = (
-        lax.all_to_all(queries, "ulysses", split_axis=1, concat_axis=0, tiled=True),
+        view_tails(queries, "ulysses", 1, 0),
         lax.all_to_all(key_rows, "ulysses", split_axis=1, concat_axis=0, tiled=True),
         lax.all_to_all(value_rows, "ulysses", split_axis=1, concat_axis=0, tiled=True),
         lax.all_to_all(grad_out, "ulysses", split_axis=1, concat_axis=0, tiled=True),

time: 216 us -> 205 us (0.949)
  waiting for transfers between devices: 69.5 us -> 64 us
  local copies, waits for them, and re-layouts: 44 us -> 41 us
    all_to_all x1 -> x0, waiting for transfers between devices: 6.77 us -> none  [body(): lax.all_to_all(queries, 'ulysses', split_axis=1, concat_axis=0, tiled=True)]
    ppermute x12, waiting for transfers between devices: 42.7 us -> 47.8 us  [swapped(): lax.ppermute(x, axis, [(i, i ^ 1 << distance) for i in range(lax.axis_siz...]
    all_to_all x1 -> x0, starting transfers between devices: 4.24 us -> none  [body(): lax.all_to_all(queries, 'ulysses', split_axis=1, concat_axis=0, tiled=True)]
    all_to_all x1, waiting for transfers between devices: 5.29 us -> 2.69 us  [body(): lax.all_to_all(value_rows, 'ulysses', split_axis=1, concat_axis=0, tiled=...]
    ppermute x0 -> x3, starting transfers between devices: none -> 2.29 us  [view_tails(): lax.ppermute(block_now, chip_axis, perm=[(to_i, to_i ^ i0) for to_i in ra...]
    unnamed x55 -> x66, local copies, waits for them, and re-layouts: 18.2 us -> 19.1 us
  transfers between devices with their start and end apart: 20 -> 22, of which waited for: 8 -> 8; matrix products, arithmetic and copies ran while one was open for 31% -> 31% of each run, Pallas kernels for 0% -> 0%
where the time goes in v1:
time: 205 us; the launch traced here: 204 us
  waiting for transfers between devices  64 us (31%)
  matrix products  50.4 us (25%)
  starting transfers between devices  44.2 us (22%)
  local copies, waits for them, and re-layouts  41 us (20%)
  other arithmetic  2.96 us (1%)
    ppermute x12, waiting for transfers between devices, swapped(): lax.ppermute(x, axis, [(i, i ^ 1 << distance) for i in range(lax.axis_siz...  47.8 us
    unnamed x66, local copies, waits for them, and re-layouts  19.1 us
    ppermute x12, starting transfers between devices, swapped(): lax.ppermute(x, axis, [(i, i ^ 1 << distance) for i in range(lax.axis_siz...  14.8 us
    dot_general x4, matrix products, block_forward(): jnp.einsum('hqk,khd->qhd', shifted.astype(jnp.bfloat16), value3, preferre...  14.4 us
    dot_general x4, matrix products, block_forward(): jnp.einsum('qhd,khd->hqk', query3, key3, preferred_element_type=jnp.float32)  8.93 us
    dot_general x4, matrix products, block_backward(): jnp.einsum('hqk,qhd->khd', probs.astype(jnp.bfloat16), grad3, preferred_e...  8.81 us
    dot_general x4, matrix products, block_backward(): jnp.einsum('hqk,qhd->khd', score_gradient, query3, preferred_element_type...  8.67 us
    ppermute x6, local copies, waits for them, and re-layouts, swapped(): lax.ppermute(x, axis, [(i, i ^ 1 << distance) for i in range(lax.axis_siz...  7.52 us
  transfers between devices with their start and end apart: 22, of which 8 were waited for; matrix products, arithmetic and copies ran while one was open for 31% of the time, Pallas kernels for 0%

profile of v1, /device:TPU:0, one launch (start us, length us, event | category | flops | bytes accessed | tf_op | source)
XLA Modules:
  0.0 203.8 jit_solution(15493550092184907213)
XLA Ops:
  0.7 2.1 %copy.236 = bf16[128,2048]{0,1:T(8,128)(2,1)} copy(bf16[128,2048]{1,0:T(8,128)(2,1)} %param.5) | data formatting | bytes 1048576 | tf_op args[1]
  2.8 4.2 %all-to-all-start = ((bf16[128,4,512]{0,2,1:T(8,128)(2,1)}), bf16[128,4,512]{0,2,1:T(8,128)(2,1)S(1)}, u32[]{:S(2)}, u32[]{:S(2)}) async-start(bf16[128,4,512]{0,2,1:T(8,128)(2,1)} %bitcast.9), calls=%async_computation | async-start | bytes 1048576 | tf_op jit(solution)/shard_map/all_to_all | solution.py:106
  7.0 2.0 %copy.240 = bf16[128,2048]{0,1:T(8,128)(2,1)} copy(bf16[128,2048]{1,0:T(8,128)(2,1)} %param.6) | data formatting | bytes 1048576 | tf_op args[2]
  9.1 6.8 %all-to-all-done = bf16[128,4,512]{0,2,1:T(8,128)(2,1)S(1)} async-done(((bf16[128,4,512]{0,2,1:T(8,128)(2,1)}), bf16[128,4,512]{0,2,1:T(8,128)(2,1)S(1)}, u32[]{:S(2)}, u32[]{:S(2)}) %all-to-all-start) | async-done | bytes 524320 | tf_op jit(solution)/shard_map/all_to_all | solution.py:106
  15.8 3.5 %all-to-all-start.1 = ((bf16[128,4,512]{0,2,1:T(8,128)(2,1)}), bf16[128,4,512]{0,2,1:T(8,128)(2,1)S(1)}, u32[]{:S(2)}, u32[]{:S(2)}) async-start(bf16[128,4,512]{0,2,1:T(8,128)(2,1)} %bitcast.11), calls=%async_computation.1 | async-start | bytes 1048576 | tf_op jit(solution)/shard_map/all_to_all | solution.py:107
  22.6 2.3 %collective-permute-start.3 = (bf16[512,512]{1,0:T(8,128)(2,1)S(1)}, bf16[512,512]{1,0:T(8,128)(2,1)}, u32[]{:S(2)}, u32[]{:S(2)}) collective-permute-start(bf16[512,512]{1,0:T(8,128)(2,1)S(1)} %bitcast.211), channel_id=1, source_target_pairs={{0,1},{1,0},{2,3},{3,2},{4,5},{5,4},{6,7},{7,6},{8,9},{9,8},{10,11... | collective-permute-start | bytes 1572872 | tf_op jit(solution)/shard_map/ppermute | solution.py:25
  26.0 2.7 %all-to-all-done.1 = bf16[128,4,512]{0,2,1:T(8,128)(2,1)S(1)} async-done(((bf16[128,4,512]{0,2,1:T(8,128)(2,1)}), bf16[128,4,512]{0,2,1:T(8,128)(2,1)S(1)}, u32[]{:S(2)}, u32[]{:S(2)}) %all-to-all-start.1) | async-done | bytes 524320 | tf_op jit(solution)/shard_map/all_to_all | solution.py:107
  28.7 3.5 %all-to-all-start.3 = ((bf16[128,4,512]{0,2,1:T(8,128)(2,1)}), bf16[128,4,512]{0,2,1:T(8,128)(2,1)S(1)}, u32[]{:S(2)}, u32[]{:S(2)}) async-start(bf16[128,4,512]{0,2,1:T(8,128)(2,1)} %bitcast.37), calls=%async_computation.3 | async-start | bytes 1048576 | tf_op jit(solution)/shard_map/all_to_all | solution.py:108
  35.4 3.3 %collective-permute-start.8 = (bf16[512,512]{1,0:T(8,128)(2,1)}, bf16[512,512]{1,0:T(8,128)(2,1)}, u32[]{:S(2)}, u32[]{:S(2)}) collective-permute-start(bf16[512,512]{1,0:T(8,128)(2,1)} %bitcast.19), channel_id=1, source_target_pairs={{0,4},{1,5},{2,6},{3,7},{4,0},{5,1},{6,2},{7,3},{8,12},{9,13},{10,... | collective-permute-start | bytes 1572872 | tf_op jit(solution)/shard_map/ppermute | solution.py:25
  42.2 2.7 %multiply_reduce_fusion.3 = (f32[4,512]{1,0:T(4,128)S(1)}, f32[4,512,512]{1,2,0:T(8,128)}) fusion(bf16[512,4,128]{0,2,1:T(8,128)(2,1)S(1)} %copy.285, bf16[512,4,128]{2,1,0:T(4,128)(2,1)S(1)} %reshape.154), kind=kOutput, calls=%fused_computation.28 | convolution fusion | flops 270530560 | bytes 5251072 | tf_op jit(solution)/shard_map/qhd,khd->hqk/dot_general | solution.py:39
  47.8 2.8 %multiply_reduce_fusion.2 = (f32[4,512]{1,0:T(4,128)S(1)}, f32[4,512,512]{1,2,0:T(8,128)}) fusion(bf16[512,4,128]{0,2,1:T(8,128)(2,1)S(1)} %copy.285, bf16[512,4,128]{0,2,1:T(8,128)(2,1)S(1)} %bitcast.198), kind=kOutput, calls=%fused_computation.27 | convolution fusion | flops 270530560 | bytes 5251072 | tf_op jit(solution)/shard_map/qhd,khd->hqk/dot_general | solution.py:39
  50.6 35.1 %collective-permute-done.5 = bf16[512,512]{1,0:T(8,128)(2,1)} collective-permute-done((bf16[512,512]{1,0:T(8,128)(2,1)S(1)}, bf16[512,512]{1,0:T(8,128)(2,1)}, u32[]{:S(2)}, u32[]{:S(2)}) %collective-permute-start.5) | collective-permute-done | bytes 524320 | tf_op jit(solution)/shard_map/ppermute | solution.py:25
  87.0 2.7 %multiply_reduce_fusion.1 = (f32[4,512]{1,0:T(4,128)S(1)}, f32[4,512,512]{1,2,0:T(8,128)}) fusion(bf16[512,4,128]{0,2,1:T(8,128)(2,1)S(1)} %copy.285, bf16[512,4,128]{0,2,1:T(8,128)(2,1)S(1)} %bitcast.200), kind=kOutput, calls=%fused_computation.26 | convolution fusion | flops 270530560 | bytes 5251072 | tf_op jit(solution)/shard_map/qhd,khd->hqk/dot_general | solution.py:39
  91.8 3.1 %copy-done.2 = f32[4,512,512]{1,2,0:T(8,128)S(1)} copy-done((f32[4,512,512]{1,2,0:T(8,128)S(1)}, f32[4,512,512]{1,2,0:T(8,128)}, u32[]{:S(2)}) %copy-start.2) | copy-done | bytes 4194328
  103.7 4.3 %fusion.74 = f32[512,4,128]{0,2,1:T(8,128)} fusion(bf16[512,4,128]{0,2,1:T(8,128)(2,1)S(1)} %bitcast.204, f32[4,512,512]{1,2,0:T(8,128)} %get-tuple-element.30, f32[4,512]{1,0:T(4,128)S(1)} %get-tuple-element.29, f32[512,4]{0,1:T(4,128)S(1)} %get-tuple-element.21), kind=kOutput, calls=%fused_computation.63 | convolution fusion | flops 271843328 | bytes 5783552 | tf_op jit(solution)/shard_map/hqk,khd->qhd/dot_general | solution.py:44
  108.1 1.8 fusion.118
  112.8 4.3 %fusion.80 = f32[512,4,128]{0,2,1:T(8,128)} fusion(bf16[512,4,128]{0,2,1:T(8,128)(2,1)S(1)} %bitcast.206, f32[4,512,512]{1,2,0:T(8,128)} %copy-done.5, f32[4,512]{1,0:T(4,128)S(1)} %get-tuple-element.27, f32[512,4]{0,1:T(4,128)S(1)} %get-tuple-element.22), kind=kOutput, calls=%fused_computation.65 | convolution fusion | flops 271843328 | bytes 5783552 | tf_op jit(solution)/shard_map/hqk,khd->qhd/dot_general | solution.py:44
  118.3 4.9 %multiply_reduce_fusion.4 = (f32[512,4]{0,1:T(4,128)S(1)}, bf16[512,4,128]{0,2,1:T(8,128)(2,1)}) fusion(bf16[512,4,128]{0,2,1:T(8,128)(2,1)S(1)} %reshape.162, f32[512,4]{0,1:T(4,128)S(1)} %get-tuple-element.16, f32[512,4,128]{0,2,1:T(8,128)} %fusion.80, f32[512,4]{0,1:T(4,128)S(1)} %get-tuple-element.19, f32[512,4,128]{0,2,1:T(8,128)} %fusion.74, ...), kind=kOutput, calls=%fused_computation.99 | convolution fusion | flops 274724864 | bytes 8962048 | tf_op jit(solution)/shard_map/hqk,khd->qhd/dot_general | solution.py:44
  135.6 2.6 %collective-permute-start.13 = (bf16[512,4,128]{2,0,1:T(8,128)(2,1)}, bf16[512,4,128]{2,0,1:T(8,128)(2,1)}, u32[]{:S(2)}, u32[]{:S(2)}) collective-permute-start(bf16[512,4,128]{2,0,1:T(8,128)(2,1)} %fusion.118), channel_id=1, source_target_pairs={{0,2},{1,3},{2,0},{3,1},{4,6},{5,7},{6,4},{7,5},{8,10},{9,11},{10,... | collective-permute-start | bytes 1572872 | tf_op jit(solution)/shard_map/ppermute | solution.py:25
  143.9 2.0 all_to_all.111
  145.9 4.1 %all-to-all-start.4 = ((bf16[4,128,512]{2,1,0:T(8,128)(2,1)}), bf16[4,128,512]{2,1,0:T(8,128)(2,1)}, u32[]{:S(2)}, u32[]{:S(2)}) async-start(bf16[4,128,512]{2,1,0:T(8,128)(2,1)} %all_to_all.111), calls=%async_computation.4 | async-start | bytes 1048576 | tf_op jit(solution)/shard_map/all_to_all | solution.py:142
  150.1 3.2 %fusion.112 = bf16[512,4,128]{0,2,1:T(8,128)(2,1)} fusion(bf16[512,4,128]{0,2,1:T(8,128)(2,1)S(1)} %copy.285, bf16[4,512,512]{1,2,0:T(8,128)(2,1)} %copy-done.10), kind=kOutput, calls=%fused_computation.91 | convolution fusion | flops 268697600 | bytes 3145728 | tf_op jit(solution)/shard_map/hqk,qhd->khd/dot_general | solution.py:79
  155.4 5.6 %collective-permute-done.14 = bf16[512,4,128]{2,0,1:T(8,128)(2,1)} collective-permute-done((bf16[512,4,128]{2,0,1:T(8,128)(2,1)}, bf16[512,4,128]{2,0,1:T(8,128)(2,1)}, u32[]{:S(2)}, u32[]{:S(2)}) %collective-permute-start.14) | collective-permute-done | bytes 524320 | tf_op jit(solution)/shard_map/ppermute | solution.py:25
  163.0 4.2 %all-to-all-start.2 = ((bf16[4,128,512]{1,2,0:T(8,128)(2,1)}), bf16[4,128,512]{1,2,0:T(8,128)(2,1)}, u32[]{:S(2)}, u32[]{:S(2)}) async-start(bf16[4,128,512]{1,2,0:T(8,128)(2,1)} %copy.260), calls=%async_computation.2 | async-start | bytes 1048576 | tf_op jit(solution)/shard_map/all_to_all | solution.py:141
  167.2 3.8 %add_convert_fusion = bf16[512,4,128]{2,0,1:T(8,128)(2,1)S(1)} fusion(bf16[512,4,128]{2,0,1:T(8,128)(2,1)} %collective-permute-done.14, bf16[512,4,128]{2,0,1:T(8,128)(2,1)} %collective-permute-done.13, bf16[512,4,128]{2,0,1:T(8,128)(2,1)} %collective-permute-done.12, bf16[512,4,128]{0,2,1:T(8,128)(2,1)S(1)} %reshape.162, ...), kind=kOutput, calls=%fused_computation.97 | convolution fusion | flops 273940480 | bytes 6823936 | tf_op jit(solution)/shard_map/hqk,qhd->khd/dot_general | solution.py:67
  172.4 3.7 %all-to-all-done.2 = bf16[4,128,512]{1,2,0:T(8,128)(2,1)} async-done(((bf16[4,128,512]{1,2,0:T(8,128)(2,1)}), bf16[4,128,512]{1,2,0:T(8,128)(2,1)}, u32[]{:S(2)}, u32[]{:S(2)}) %all-to-all-start.2) | async-done | bytes 524320 | tf_op jit(solution)/shard_map/all_to_all | solution.py:141
  176.1 4.1 %all-to-all-start.6 = ((bf16[4,128,512]{2,1,0:T(8,128)(2,1)}), bf16[4,128,512]{2,1,0:T(8,128)(2,1)}, u32[]{:S(2)}, u32[]{:S(2)}) async-start(bf16[4,128,512]{2,1,0:T(8,128)(2,1)} %all_to_all.119), calls=%async_computation.6 | async-start | bytes 1048576 | tf_op jit(solution)/shard_map/all_to_all | solution.py:156
  180.2 7.0 %collective-permute-done.11 = bf16[512,4,128]{0,2,1:T(8,128)(2,1)} collective-permute-done((bf16[512,4,128]{0,2,1:T(8,128)(2,1)}, bf16[512,4,128]{0,2,1:T(8,128)(2,1)}, u32[]{:S(2)}, u32[]{:S(2)}) %collective-permute-start.11) | collective-permute-done | bytes 524320 | tf_op jit(solution)/shard_map/ppermute | solution.py:25
  187.3 2.2 %add_convert_fusion.1 = bf16[512,4,128]{0,2,1:T(8,128)(2,1)S(1)} fusion(bf16[512,4,128]{0,2,1:T(8,128)(2,1)} %collective-permute-done.11, bf16[512,4,128]{0,2,1:T(8,128)(2,1)} %collective-permute-done.10, bf16[512,4,128]{0,2,1:T(8,128)(2,1)} %collective-permute-done.9, bf16[512,4,128]{0,2,1:T(8,128)(2,1)S(1)} %copy.285, bf16[4,512,512]{1,2,0:T(8,128)(2,1)S(1)} %copy-done.12), kind=kOutput, calls=%fused_computation.98 | convolution fusion | flops 270794752 | bytes 4718592 | tf_op jit(solution)/shard_map/hqk,qhd->khd/dot_general | solution.py:79
  190.5 3.5 %all-to-all-start.5 = ((bf16[4,128,512]{1,2,0:T(8,128)(2,1)}), bf16[4,128,512]{1,2,0:T(8,128)(2,1)S(1)}, u32[]{:S(2)}, u32[]{:S(2)}) async-start(bf16[4,128,512]{1,2,0:T(8,128)(2,1)} %copy.293), calls=%async_computation.5 | async-start | bytes 1048576 | tf_op jit(solution)/shard_map/all_to_all | solution.py:149
  196.3 2.0 %copy.300 = bf16[128,2048]{1,0:T(8,128)(2,1)} copy(bf16[128,2048]{0,1:T(8,128)(2,1)} %bitcast.36) | data formatting | bytes 1048576
  200.7 2.1 %all-to-all-done.5 = bf16[4,128,512]{1,2,0:T(8,128)(2,1)S(1)} async-done(((bf16[4,128,512]{1,2,0:T(8,128)(2,1)}), bf16[4,128,512]{1,2,0:T(8,128)(2,1)S(1)}, u32[]{:S(2)}, u32[]{:S(2)}) %all-to-all-start.5) | async-done | bytes 524320 | tf_op jit(solution)/shard_map/all_to_all | solution.py:149
  (140 shorter events, 60.3 us)
Async XLA Ops:
  0.6 18.7 %copy-start.27 = (bf16[128,2048]{1,0:T(8,128)(2,1)S(1)}, bf16[128,2048]{1,0:T(8,128)(2,1)}, u32[]{:S(2)}) copy-start(bf16[128,2048]{1,0:T(8,128)(2,1)} %param.4) | copy-start | bytes 1572868
  0.6 24.3 %copy-start.28 = (bf16[128,2048]{1,0:T(8,128)(2,1)S(1)}, bf16[128,2048]{1,0:T(8,128)(2,1)}, u32[]{:S(2)}) copy-start(bf16[128,2048]{1,0:T(8,128)(2,1)} %param.7) | copy-start | bytes 1572868
  2.8 13.1 %all-to-all-start = ((bf16[128,4,512]{0,2,1:T(8,128)(2,1)}), bf16[128,4,512]{0,2,1:T(8,128)(2,1)S(1)}, u32[]{:S(2)}, u32[]{:S(2)}) async-start(bf16[128,4,512]{0,2,1:T(8,128)(2,1)} %bitcast.9), calls=%async_computation | async-start | bytes 1048576 | tf_op jit(solution)/shard_map/all_to_all | solution.py:106
  15.8 12.8 %all-to-all-start.1 = ((bf16[128,4,512]{0,2,1:T(8,128)(2,1)}), bf16[128,4,512]{0,2,1:T(8,128)(2,1)S(1)}, u32[]{:S(2)}, u32[]{:S(2)}) async-start(bf16[128,4,512]{0,2,1:T(8,128)(2,1)} %bitcast.11), calls=%async_computation.1 | async-start | bytes 1048576 | tf_op jit(solution)/shard_map/all_to_all | solution.py:107
  19.8 12.3 %collective-permute-start = (bf16[128,512]{1,0:T(8,128)(2,1)S(1)}, bf16[128,512]{1,0:T(8,128)(2,1)S(1)}, u32[]{:S(2)}, u32[]{:S(2)}) collective-permute-start(bf16[128,512]{1,0:T(8,128)(2,1)S(1)} %bitcast.225), channel_id=1, source_target_pairs={{0,8},{8,0},{16,24},{24,16},{1,9},{9,1},{17,25},{25,17},{2,10},{10... | collective-permute-start | bytes 393224 | tf_op jit(solution)/shard_map/ppermute | solution.py:96
  20.4 11.7 %collective-permute-start.1 = (bf16[128,512]{1,0:T(8,128)(2,1)S(1)}, bf16[128,512]{1,0:T(8,128)(2,1)S(1)}, u32[]{:S(2)}, u32[]{:S(2)}) collective-permute-start(bf16[128,512]{1,0:T(8,128)(2,1)S(1)} %bitcast.226), channel_id=1, source_target_pairs={{0,16},{8,24},{16,0},{24,8},{1,17},{9,25},{17,1},{25,9},{2,18},{10... | collective-permute-start | bytes 393224 | tf_op jit(solution)/shard_map/ppermute | solution.py:96
  22.3 10.9 %collective-permute-start.2 = (bf16[128,512]{1,0:T(8,128)(2,1)S(1)}, bf16[128,512]{1,0:T(8,128)(2,1)S(1)}, u32[]{:S(2)}, u32[]{:S(2)}) collective-permute-start(bf16[128,512]{1,0:T(8,128)(2,1)S(1)} %bitcast.227), channel_id=1, source_target_pairs={{0,24},{8,16},{16,8},{24,0},{1,25},{9,17},{17,9},{25,1},{2,26},{10... | collective-permute-start | bytes 393224 | tf_op jit(solution)/shard_map/ppermute | solution.py:96
  22.6 23.6 %collective-permute-start.3 = (bf16[512,512]{1,0:T(8,128)(2,1)S(1)}, bf16[512,512]{1,0:T(8,128)(2,1)}, u32[]{:S(2)}, u32[]{:S(2)}) collective-permute-start(bf16[512,512]{1,0:T(8,128)(2,1)S(1)} %bitcast.211), channel_id=1, source_target_pairs={{0,1},{1,0},{2,3},{3,2},{4,5},{5,4},{6,7},{7,6},{8,9},{9,8},{10,11... | collective-permute-start | bytes 1572872 | tf_op jit(solution)/shard_map/ppermute | solution.py:25
  28.7 16.9 %all-to-all-start.3 = ((bf16[128,4,512]{0,2,1:T(8,128)(2,1)}), bf16[128,4,512]{0,2,1:T(8,128)(2,1)S(1)}, u32[]{:S(2)}, u32[]{:S(2)}) async-start(bf16[128,4,512]{0,2,1:T(8,128)(2,1)} %bitcast.37), calls=%async_computation.3 | async-start | bytes 1048576 | tf_op jit(solution)/shard_map/all_to_all | solution.py:108
  34.4 11.1 %copy-start.13 = (bf16[512,4,128]{2,1,0:T(4,128)(2,1)}, bf16[512,4,128]{2,1,0:T(4,128)(2,1)S(1)}, u32[]{:S(2)}) copy-start(bf16[512,4,128]{2,1,0:T(4,128)(2,1)S(1)} %reshape.154) | copy-start | bytes 1572868
  35.4 76.1 %collective-permute-start.8 = (bf16[512,512]{1,0:T(8,128)(2,1)}, bf16[512,512]{1,0:T(8,128)(2,1)}, u32[]{:S(2)}, u32[]{:S(2)}) collective-permute-start(bf16[512,512]{1,0:T(8,128)(2,1)} %bitcast.19), channel_id=1, source_target_pairs={{0,4},{1,5},{2,6},{3,7},{4,0},{5,1},{6,2},{7,3},{8,12},{9,13},{10,... | collective-permute-start | bytes 1572872 | tf_op jit(solution)/shard_map/ppermute | solution.py:25
  38.7 63.8 %collective-permute-start.6 = (bf16[512,512]{1,0:T(8,128)(2,1)}, bf16[512,512]{1,0:T(8,128)(2,1)}, u32[]{:S(2)}, u32[]{:S(2)}) collective-permute-start(bf16[512,512]{1,0:T(8,128)(2,1)} %bitcast.19), channel_id=1, source_target_pairs={{0,2},{1,3},{2,0},{3,1},{4,6},{5,7},{6,4},{7,5},{8,10},{9,11},{10,... | collective-permute-start | bytes 1572872 | tf_op jit(solution)/shard_map/ppermute | solution.py:25
  40.2 76.8 %collective-permute-start.4 = (bf16[512,512]{1,0:T(8,128)(2,1)}, bf16[512,512]{1,0:T(8,128)(2,1)}, u32[]{:S(2)}, u32[]{:S(2)}) collective-permute-start(bf16[512,512]{1,0:T(8,128)(2,1)} %bitcast.19), channel_id=1, source_target_pairs={{0,1},{1,0},{2,3},{3,2},{4,5},{5,4},{6,7},{7,6},{8,9},{9,8},{10,11... | collective-permute-start | bytes 1572872 | tf_op jit(solution)/shard_map/ppermute | solution.py:25
  41.8 44.0 %collective-permute-start.5 = (bf16[512,512]{1,0:T(8,128)(2,1)S(1)}, bf16[512,512]{1,0:T(8,128)(2,1)}, u32[]{:S(2)}, u32[]{:S(2)}) collective-permute-start(bf16[512,512]{1,0:T(8,128)(2,1)S(1)} %bitcast.212), channel_id=1, source_target_pairs={{0,2},{1,3},{2,0},{3,1},{4,6},{5,7},{6,4},{7,5},{8,10},{9,11},{10,... | collective-permute-start | bytes 1572872 | tf_op jit(solution)/shard_map/ppermute | solution.py:25
  45.5 56.0 %copy-start.17 = (bf16[512,4,128]{0,2,1:T(8,128)(2,1)}, bf16[512,4,128]{0,2,1:T(8,128)(2,1)S(1)}, u32[]{:S(2)}) copy-start(bf16[512,4,128]{0,2,1:T(8,128)(2,1)S(1)} %reshape.155) | copy-start | bytes 1572868
  46.2 43.6 %collective-permute-start.7 = (bf16[512,512]{1,0:T(8,128)(2,1)S(1)}, bf16[512,512]{1,0:T(8,128)(2,1)}, u32[]{:S(2)}, u32[]{:S(2)}) collective-permute-start(bf16[512,512]{1,0:T(8,128)(2,1)S(1)} %bitcast.213), channel_id=1, source_target_pairs={{0,4},{1,5},{2,6},{3,7},{4,0},{5,1},{6,2},{7,3},{8,12},{9,13},{10,... | collective-permute-start | bytes 1572872 | tf_op jit(solution)/shard_map/ppermute | solution.py:25
  47.8 41.9 %copy-start.15 = (bf16[512,512]{0,1:T(8,128)(2,1)}, bf16[512,512]{0,1:T(8,128)(2,1)S(1)}, u32[]{:S(2)}) copy-start(bf16[512,512]{0,1:T(8,128)(2,1)S(1)} %copy.245) | copy-start | bytes 1572868
  112.7 10.5 %copy-start.25 = (bf16[512,512]{0,1:T(8,128)(2,1)}, bf16[512,512]{0,1:T(8,128)(2,1)S(1)}, u32[]{:S(2)}) copy-start(bf16[512,512]{0,1:T(8,128)(2,1)S(1)} %copy.258) | copy-start | bytes 1572868
  125.5 16.0 %copy-start.10 = (bf16[4,512,512]{1,2,0:T(8,128)(2,1)}, bf16[4,512,512]{1,2,0:T(8,128)(2,1)S(1)}, u32[]{:S(2)}) copy-start(bf16[4,512,512]{1,2,0:T(8,128)(2,1)S(1)} %multiply_convert_fusion.2) | copy-start | bytes 6291460
  132.3 8.3 %copy-start.11 = (bf16[4,512,512]{1,2,0:T(8,128)(2,1)}, bf16[4,512,512]{1,2,0:T(8,128)(2,1)S(1)}, u32[]{:S(2)}) copy-start(bf16[4,512,512]{1,2,0:T(8,128)(2,1)S(1)} %multiply_convert_fusion.3) | copy-start | bytes 6291460
  132.3 7.4 %copy-start.14 = (bf16[512,4,128]{2,1,0:T(4,128)(2,1)S(1)}, bf16[512,4,128]{2,1,0:T(4,128)(2,1)}, u32[]{:S(2)}) copy-start(bf16[512,4,128]{2,1,0:T(4,128)(2,1)} %copy-done.13) | copy-start | bytes 1572868
  134.9 26.1 %collective-permute-start.14 = (bf16[512,4,128]{2,0,1:T(8,128)(2,1)}, bf16[512,4,128]{2,0,1:T(8,128)(2,1)}, u32[]{:S(2)}, u32[]{:S(2)}) collective-permute-start(bf16[512,4,128]{2,0,1:T(8,128)(2,1)} %fusion.115), channel_id=1, source_target_pairs={{0,4},{1,5},{2,6},{3,7},{4,0},{5,1},{6,2},{7,3},{8,12},{9,13},{10,... | collective-permute-start | bytes 1572872 | tf_op jit(solution)/shard_map/ppermute | solution.py:25
  135.6 31.6 %collective-permute-start.13 = (bf16[512,4,128]{2,0,1:T(8,128)(2,1)}, bf16[512,4,128]{2,0,1:T(8,128)(2,1)}, u32[]{:S(2)}, u32[]{:S(2)}) collective-permute-start(bf16[512,4,128]{2,0,1:T(8,128)(2,1)} %fusion.118), channel_id=1, source_target_pairs={{0,2},{1,3},{2,0},{3,1},{4,6},{5,7},{6,4},{7,5},{8,10},{9,11},{10,... | collective-permute-start | bytes 1572872 | tf_op jit(solution)/shard_map/ppermute | solution.py:25
  138.2 29.1 %collective-permute-start.12 = (bf16[512,4,128]{2,0,1:T(8,128)(2,1)}, bf16[512,4,128]{2,0,1:T(8,128)(2,1)}, u32[]{:S(2)}, u32[]{:S(2)}) collective-permute-start(bf16[512,4,128]{2,0,1:T(8,128)(2,1)} %fusion.121), channel_id=1, source_target_pairs={{0,1},{1,0},{2,3},{3,2},{4,5},{5,4},{6,7},{7,6},{8,9},{9,8},{10,11... | collective-permute-start | bytes 1572872 | tf_op jit(solution)/shard_map/ppermute | solution.py:25
  145.9 17.1 %all-to-all-start.4 = ((bf16[4,128,512]{2,1,0:T(8,128)(2,1)}), bf16[4,128,512]{2,1,0:T(8,128)(2,1)}, u32[]{:S(2)}, u32[]{:S(2)}) async-start(bf16[4,128,512]{2,1,0:T(8,128)(2,1)} %all_to_all.111), calls=%async_computation.4 | async-start | bytes 1048576 | tf_op jit(solution)/shard_map/all_to_all | solution.py:142
  153.3 26.9 %collective-permute-start.9 = (bf16[512,4,128]{0,2,1:T(8,128)(2,1)}, bf16[512,4,128]{0,2,1:T(8,128)(2,1)}, u32[]{:S(2)}, u32[]{:S(2)}) collective-permute-start(bf16[512,4,128]{0,2,1:T(8,128)(2,1)} %fusion.112), channel_id=1, source_target_pairs={{0,1},{1,0},{2,3},{3,2},{4,5},{5,4},{6,7},{7,6},{8,9},{9,8},{10,11... | collective-permute-start | bytes 1572872 | tf_op jit(solution)/shard_map/ppermute | solution.py:25
  155.4 24.8 %collective-permute-start.10 = (bf16[512,4,128]{0,2,1:T(8,128)(2,1)}, bf16[512,4,128]{0,2,1:T(8,128)(2,1)}, u32[]{:S(2)}, u32[]{:S(2)}) collective-permute-start(bf16[512,4,128]{0,2,1:T(8,128)(2,1)} %fusion.113), channel_id=1, source_target_pairs={{0,2},{1,3},{2,0},{3,1},{4,6},{5,7},{6,4},{7,5},{8,10},{9,11},{10,... | collective-permute-start | bytes 1572872 | tf_op jit(solution)/shard_map/ppermute | solution.py:25
  161.0 26.3 %collective-permute-start.11 = (bf16[512,4,128]{0,2,1:T(8,128)(2,1)}, bf16[512,4,128]{0,2,1:T(8,128)(2,1)}, u32[]{:S(2)}, u32[]{:S(2)}) collective-permute-start(bf16[512,4,128]{0,2,1:T(8,128)(2,1)} %fusion.114), channel_id=1, source_target_pairs={{0,4},{1,5},{2,6},{3,7},{4,0},{5,1},{6,2},{7,3},{8,12},{9,13},{10,... | collective-permute-start | bytes 1572872 | tf_op jit(solution)/shard_map/ppermute | solution.py:25
  163.0 13.0 %all-to-all-start.2 = ((bf16[4,128,512]{1,2,0:T(8,128)(2,1)}), bf16[4,128,512]{1,2,0:T(8,128)(2,1)}, u32[]{:S(2)}, u32[]{:S(2)}) async-start(bf16[4,128,512]{1,2,0:T(8,128)(2,1)} %copy.260), calls=%async_computation.2 | async-start | bytes 1048576 | tf_op jit(solution)/shard_map/all_to_all | solution.py:141
  167.2 20.1 %copy-start.12 = (bf16[4,512,512]{1,2,0:T(8,128)(2,1)S(1)}, bf16[4,512,512]{1,2,0:T(8,128)(2,1)}, u32[]{:S(2)}) copy-start(bf16[4,512,512]{1,2,0:T(8,128)(2,1)} %copy-done.11) | copy-start | bytes 6291460
  176.1 14.5 %all-to-all-start.6 = ((bf16[4,128,512]{2,1,0:T(8,128)(2,1)}), bf16[4,128,512]{2,1,0:T(8,128)(2,1)}, u32[]{:S(2)}, u32[]{:S(2)}) async-start(bf16[4,128,512]{2,1,0:T(8,128)(2,1)} %all_to_all.119), calls=%async_computation.6 | async-start | bytes 1048576 | tf_op jit(solution)/shard_map/all_to_all | solution.py:156
  190.5 12.3 %all-to-all-start.5 = ((bf16[4,128,512]{1,2,0:T(8,128)(2,1)}), bf16[4,128,512]{1,2,0:T(8,128)(2,1)S(1)}, u32[]{:S(2)}, u32[]{:S(2)}) async-start(bf16[4,128,512]{1,2,0:T(8,128)(2,1)} %copy.293), calls=%async_computation.5 | async-start | bytes 1048576 | tf_op jit(solution)/shard_map/all_to_all | solution.py:149
  (19 other events, 77.1 us)
